TPU v7x, 128 devices: a whole 4x4x4 slice. The times are simulated.
128 devices in a mesh: row: 8 (over x_lo, z), col: 16 (over y, x_hi, core).
Axes of the slice: x: 4 (x_hi: 2, x_lo: 2; x = x_hi * 2 + x_lo), y: 4, z: 4, core: 2. Of those that a mesh axis runs over, the one named last changes fastest.
Arguments:
- amplitudes: bfloat16 [32, 32, 12, 4096], P('row', 'col'), may hold values from -6 to 6
- integrals: bfloat16 [32, 32, 47, 4096], P('row', 'col'), may hold values from -0.125 to 0.125
- pair_lists: int32 [8, 12, 2], replicated, may hold values from 0 to 46, as said below
- tile_counts: int32 [8], replicated, may hold values from 1 to 12, as said below
Outputs:
- symmetric: float32 [32, 32, 12, 4096], P('row', 'col')
Inputs may be any that keep to these rules, and one draw needn't show every extreme that they name: `pair_lists`: each grid row lists 12 distinct ordered pairs of different tiles. `tile_counts`: the largest count equals 12.
All inputs are finite; a program needn't handle non-finite values.
Results may differ from a plain program's by a relative error of at most 0.0029.
Values may be sent and summed in bfloat16 or wider, within the bound.
A program may use at most 128 MiB of HBM per device.

v0:
```python
import jax
import jax.numpy as jnp
from jax import lax
from jax.sharding import PartitionSpec as P

TILE = 64


def spread(block, axis, owner):
    block = jnp.where(lax.axis_index(axis) == owner, block, jnp.zeros_like(block))
    return lax.psum(block, axis)


def on_device(amplitudes, integrals, pair_lists, tile_counts):
    occ_row, occ_col, slot_count, square = amplitudes.shape
    tile_width = TILE
    row_devices = lax.axis_size("row")
    col_devices = lax.axis_size("col")
    col_ratio = col_devices // row_devices
    my_row = lax.axis_index("row")
    my_col = lax.axis_index("col")
    partner_row = my_col // col_ratio
    tile_first = pair_lists[:, :, 0]
    tile_second = pair_lists[:, :, 1]
    packed = jnp.take(integrals, tile_second.reshape(-1), axis=2)
    packed = packed.reshape(occ_row, occ_col, row_devices, slot_count, square)
    received = lax.all_to_all(packed, "row", split_axis=2, concat_axis=0, tiled=True)
    received = received.reshape(occ_row * row_devices, occ_col, slot_count, square)
    piece = lax.all_gather(amplitudes, "col", axis=1, tiled=True)
    piece_count = piece.shape[1]
    left_tiles = piece.reshape(occ_row, piece_count, slot_count, tile_width, tile_width)
    right_tiles = received.reshape(piece_count, occ_col, slot_count, tile_width, tile_width)
    cycle_sum = jnp.einsum(
        "iksac,kjscb->ijsab", left_tiles, right_tiles, preferred_element_type=jnp.float32
    )
    my_count = lax.dynamic_index_in_dim(tile_counts, my_row, 0, keepdims=False)
    live_slots = (jnp.arange(slot_count, dtype=jnp.int32) < my_count).astype(jnp.float32)
    cycle_value = (cycle_sum * live_slots[None, None, :, None, None]).astype(jnp.bfloat16)
    cycle = cycle_value.reshape(occ_row, occ_col, slot_count, square)
    residual_strip = lax.all_gather(cycle, "col", axis=1, tiled=True)
    mirror_part = lax.dynamic_slice_in_dim(residual_strip, my_col % col_ratio * occ_col, occ_col, 0)
    mirror_whole = spread(mirror_part, "row", partner_row)
    mirror_block = lax.dynamic_slice_in_dim(mirror_whole, my_row * occ_row, occ_row, 1)
    mirror_block = mirror_block.reshape(occ_col, occ_row, slot_count, tile_width, tile_width)
    mine_first = lax.dynamic_index_in_dim(tile_first, my_row, 0, keepdims=False)
    mine_second = lax.dynamic_index_in_dim(tile_second, my_row, 0, keepdims=False)
    their_first = lax.dynamic_index_in_dim(tile_first, partner_row, 0, keepdims=False)
    their_second = lax.dynamic_index_in_dim(tile_second, partner_row, 0, keepdims=False)
    pair_match = (
        (mine_first[:, None] == their_second[None, :])
        & (mine_second[:, None] == their_first[None, :])
    ).astype(jnp.bfloat16)
    crossed = jnp.einsum(
        "st,jitba->ijsab", pair_match, mirror_block, preferred_element_type=jnp.float32
    )
    own_part = cycle_value.astype(jnp.float32)
    symmetric = (own_part + crossed) * live_slots[None, None, :, None, None]
    return symmetric.reshape(occ_row, occ_col, slot_count, square)


def solution(mesh):
    return jax.shard_map(
        on_device,
        mesh=mesh,
        in_specs=(P("row", "col", None, None), P("row", "col", None, None), P(), P()),
        out_specs=P("row", "col", None, None),
        check_vma=False,
    )
```

profile of v0, /device:TPU:1, one launch (start us, length us, event | category | flops | bytes accessed | tf_op | source)
XLA Modules:
  0.0 507.0 jit_solution(17754718859662884650)
XLA Ops:
  6.5 0.0 copy-start
  6.5 2.8 copy.18
  9.3 0.0 all-gather.3.cloned.1.call-update
  9.3 0.8 fusion.29
  10.1 0.1 reshape_squeeze.6
  10.2 0.0 copy-done
  10.2 15.2 %gather_fusion = bf16[96,4,2,4096]{3,2,1,0:T(2,128)(2,1)} fusion(bf16[4,2,47,4096]{3,1,2,0:T(2,128)(2,1)S(1)} %copy-done, s32[1024]{0:T(1024)S(1)} %pad_clamp_fusion), kind=kCustom, calls=%fused_computation | custom fusion | bytes 12583296 | tf_op jit(solution)/shard_map/jit(_take)/gather | solution.py:25
  25.5 8.5 %broadcast_select_fusion.1 = bf16[4,2,8,12,4096]{4,1,3,0,2:T(2,128)(2,1)} fusion(pred[8,12]{1,0:T(8,128)(4,1)S(1)} %compare_and_fusion, bf16[4,2,8,12,4096]{4,1,0,3,2:T(2,128)(2,1)} %bitcast.67), kind=kLoop, calls=%fused_computation.5 | loop fusion | flops 3145728 | bytes 12583008 | tf_op jit(solution)/shard_map/jit(_take)/select_n | solution.py:25
  33.9 6.9 %all-to-all-start = ((bf16[4,2,8,12,4096]{4,1,3,0,2:T(2,128)(2,1)}), bf16[4,2,8,12,4096]{4,1,3,0,2:T(2,128)(2,1)}, u32[]{:S(2)}, u32[]{:S(2)}) async-start(bf16[4,2,8,12,4096]{4,1,3,0,2:T(2,128)(2,1)} %broadcast_select_fusion.1), calls=%async_computation | async-start | bytes 12582912 | tf_op jit(solution)/shard_map/all_to_all | solution.py:27
  40.9 0.2 all-gather.5.cloned.1.call-start
  41.1 0.6 dynamic_slice.23
  41.7 0.6 compare_convert_fusion
  42.3 101.4 %all-to-all-done = bf16[4,2,8,12,4096]{4,1,3,0,2:T(2,128)(2,1)} async-done(((bf16[4,2,8,12,4096]{4,1,3,0,2:T(2,128)(2,1)}), bf16[4,2,8,12,4096]{4,1,3,0,2:T(2,128)(2,1)}, u32[]{:S(2)}, u32[]{:S(2)}) %all-to-all-start) | async-done | bytes 6291488 | tf_op jit(solution)/shard_map/all_to_all | solution.py:27
  143.6 20.6 %reshape_reshape.3 = bf16[32,2,12,64,64]{4,3,1,2,0:T(8,128)(2,1)} reshape(bf16[8,4,2,1,12,4096]{5,2,4,1,0,3:T(2,128)(2,1)} %bitcast.5) | data formatting | bytes 12582912 | tf_op jit(solution)/shard_map/reshape;reshape | solution.py:32
  164.2 14.4 %copy.19 = bf16[4,32,12,4096]{3,1,0,2:T(8,128)(2,1)} copy(bf16[4,32,12,4096]{3,0,2,1:T(4,128)(2,1)} %all-gather.3.cloned.1.call-done) | data formatting | bytes 25165824 | tf_op jit(solution)/shard_map/all_gather | solution.py:29
  178.6 34.4 %reshape.81 = bf16[4,32,12,64,64,1]{4,3,1,0,2,5:T(8,128)(2,1)} reshape(bf16[4,32,12,4096]{3,1,0,2:T(8,128)(2,1)} %copy.19) | data formatting | bytes 25165824 | tf_op jit(solution)/shard_map/reshape | solution.py:31
  213.0 19.0 %fusion.11 = bf16[4,2,12,64,64]{3,4,0,1,2:T(8,128)(2,1)S(1)} fusion(f32[12]{0:T(128)S(1)} %compare_convert_fusion, bf16[4,32,12,64,64,1]{4,3,1,0,2,5:T(8,128)(2,1)} %reshape.81, bf16[32,2,12,64,64]{4,3,1,2,0:T(8,128)(2,1)} %reshape_reshape.3), kind=kOutput, calls=%fused_computation.12 | convolution fusion | flops 1611399168 | bytes 19660848 | tf_op jit(solution)/shard_map/iksac,kjscb->ijsab/dot_general | solution.py:33
  232.1 1.8 copy.33
  233.8 3.7 reshape.85
  237.5 0.0 all-gather.5.cloned.1.call-update
  237.5 0.3 all-reduce.2.cloned.1.call-start
  237.8 93.1 %all-gather.5.cloned.1.call-done = bf16[4,32,12,4096]{3,0,2,1:T(4,128)(2,1)} async-done(((bf16[4,2,12,4096]{3,0,2,1:T(4,128)(2,1)}), bf16[4,32,12,4096]{3,0,2,1:T(4,128)(2,1)}) %all-gather.5.cloned.1.call-update) | async-done | bytes 12582928 | tf_op jit(solution)/shard_map/all_gather | solution.py:40
  330.9 10.8 %broadcast_select_fusion = bf16[2,32,12,4096]{3,0,2,1:T(2,128)(2,1)} fusion(pred[]{:T(512)S(6)} %eq.39, bf16[4,32,12,4096]{3,0,2,1:T(4,128)(2,1)} %all-gather.5.cloned.1.call-done, s32[]{:T(128)S(6)} %select_n.65), kind=kLoop, calls=%fused_computation.4 | loop fusion | flops 3145728 | bytes 12582917 | tf_op jit(solution)/shard_map/jit(_where)/select_n | solution.py:10
  341.7 0.0 all-reduce.2.cloned.1.call-update
  341.7 142.5 %all-reduce.2.cloned.1.call-done = bf16[2,32,12,4096]{3,0,2,1:T(2,128)(2,1)} async-done(((bf16[2,32,12,4096]{3,0,2,1:T(2,128)(2,1)}), bf16[2,32,12,4096]{3,0,2,1:T(2,128)(2,1)}) %all-reduce.2.cloned.1.call-update) | async-done | bytes 6291472 | tf_op jit(solution)/shard_map/psum | solution.py:11
  484.3 2.0 constant_dynamic-slice_fusion.4
  486.3 1.0 reshape.86
  487.3 1.1 fusion.5
  488.4 0.0 copy-start.1
  488.4 4.3 fusion.3
  492.7 3.6 copy.26
  496.3 4.2 reshape.71
  (12 shorter events, 0.1 us)
Async XLA Ops:
  6.5 3.7 copy-start
  6.5 157.7 %all-gather.3.cloned.1.call-start = ((), (), s32[]{:S(2)}) async-start(), calls=%async_computation.1 | async-start | bytes 13369344 | tf_op jit(solution)/shard_map/all_gather | solution.py:29
  33.9 7.2 %copy-start.3 = (s32[8]{0:T(128)S(1)}, s32[8]{0:T(128)}, u32[]{:S(2)}) copy-start(s32[8]{0:T(128)} %param.7) | copy-start | bytes 100
  33.9 109.7 %all-to-all-start = ((bf16[4,2,8,12,4096]{4,1,3,0,2:T(2,128)(2,1)}), bf16[4,2,8,12,4096]{4,1,3,0,2:T(2,128)(2,1)}, u32[]{:S(2)}, u32[]{:S(2)}) async-start(bf16[4,2,8,12,4096]{4,1,3,0,2:T(2,128)(2,1)} %broadcast_select_fusion.1), calls=%async_computation | async-start | bytes 12582912 | tf_op jit(solution)/shard_map/all_to_all | solution.py:27
  40.9 290.0 %all-gather.5.cloned.1.call-start = ((), (), s32[]{:S(2)}) async-start(), calls=%async_computation.2 | async-start | bytes 13369344 | tf_op jit(solution)/shard_map/all_gather | solution.py:40
  232.0 109.6 %copy-start.2 = (bf16[4,2,12,64,64]{3,4,0,1,2:T(8,128)(2,1)}, bf16[4,2,12,64,64]{3,4,0,1,2:T(8,128)(2,1)S(1)}, u32[]{:S(2)}) copy-start(bf16[4,2,12,64,64]{3,4,0,1,2:T(8,128)(2,1)S(1)} %fusion.11) | copy-start | bytes 2359300
  237.5 246.7 %all-reduce.2.cloned.1.call-start = ((), (), s32[]{:S(2)}) async-start(), calls=%async_computation.3 | async-start | bytes 12582912 | tf_op jit(solution)/shard_map/psum | solution.py:11
  488.4 12.0 %copy-start.1 = (bf16[4,2,47,4096]{3,1,2,0:T(2,128)(2,1)S(1)}, bf16[4,2,47,4096]{3,1,2,0:T(2,128)(2,1)}, u32[]{:S(2)}) copy-start(bf16[4,2,47,4096]{3,1,2,0:T(2,128)(2,1)} %param.5) | copy-start | bytes 9240580
Sparse Core Ops, SparseCore 0:
  9.8 128.3 all-gather.2
  237.6 93.2 all-gather.4
  341.8 142.4 all-reduce.1
where the time goes:
time: 509 us; the launch traced here: 507 us
  waiting for transfers between devices  337 us (66%)
  local copies, waits for them, and re-layouts  105 us (21%)
  other arithmetic  24.1 us (5%)
  matrix products  20.1 us (4%)
  between operations  13.2 us (3%)
  starting transfers between devices  7.4 us (1%)
    psum x1, waiting for transfers between devices, spread(): return lax.psum(block, axis)  143 us
    all_to_all x1, waiting for transfers between devices, on_device(): lax.all_to_all(packed, 'row', split_axis=2, concat_axis=0, tiled=True)  101 us
    all_gather x1, waiting for transfers between devices, on_device(): residual_strip = lax.all_gather(cycle, 'col', axis=1, tiled=True)  93.1 us
    reshape x1, local copies, waits for them, and re-layouts, on_device(): piece.reshape(occ_row, piece_count, slot_count, tile_width, tile_width)  34.4 us
    another operation x1, local copies, waits for them, and re-layouts, on_device(): received.reshape(piece_count, occ_col, slot_count, tile_width, tile_width)  20.6 us
    dot_general x1, matrix products, on_device(): jnp.einsum('iksac,kjscb->ijsab', left_tiles, right_tiles, preferred_eleme...  19 us
    gather x1, local copies, waits for them, and re-layouts, on_device(): packed = jnp.take(integrals, tile_second.reshape(-1), axis=2)  15.2 us
    all_gather x1, local copies, waits for them, and re-layouts, on_device(): piece = lax.all_gather(amplitudes, 'col', axis=1, tiled=True)  14.4 us
  transfers between devices with their start and end apart: 4, of which 3 were waited for; matrix products, arithmetic and copies ran while one was open for 9% of the time, Pallas kernels for 0%

commit v1 on v0

--- a/solution.py
+++ b/solution.py
@@ -26,7 +26,9 @@
     packed = packed.reshape(occ_row, occ_col, row_devices, slot_count, square)
     received = lax.all_to_all(packed, "row", split_axis=2, concat_axis=0, tiled=True)
     received = received.reshape(occ_row * row_devices, occ_col, slot_count, square)
-    piece = lax.all_gather(amplitudes, "col", axis=1, tiled=True)
+    piece = jnp.concatenate(
+        lax.all_to_all(jnp.stack([amplitudes] * lax.axis_size("col")), "col", 0, 0), axis=1
+    )
     piece_count = piece.shape[1]
     left_tiles = piece.reshape(occ_row, piece_count, slot_count, tile_width, tile_width)
     right_tiles = received.reshape(piece_count, occ_col, slot_count, tile_width, tile_width)

time: 509 us -> 616 us (1.21)
  waiting for transfers between devices: 337 us -> 419 us
  local copies, waits for them, and re-layouts: 105 us -> 121 us
  starting transfers between devices: 7.4 us -> 15.1 us
    all_to_all x0 -> x1, waiting for transfers between devices: none -> 119 us  [on_device(): lax.all_to_all(jnp.stack([amplitudes] * lax.axis_size('col')), 'col', 0, 0)]
    another operation x0 -> x2, local copies, waits for them, and re-layouts: none -> 52.6 us  [the longest x1 40.1 us: on_device(): piece.reshape(occ_row, piece_count, slot_count, tile_width, tile_width)]
    all_to_all x1, waiting for transfers between devices: 101 us -> 70.4 us  [on_device(): lax.all_to_all(packed, 'row', split_axis=2, concat_axis=0, tiled=True)]
    reshape x1, local copies, waits for them, and re-layouts: 34.4 us -> 13.2 us  [on_device(): jnp.concatenate(lax.all_to_all(jnp.stack([amplitudes] * lax.axis_size('co...]
    all_gather x1 -> x0, local copies, waits for them, and re-layouts: 14.4 us -> none  [on_device(): piece = lax.all_gather(amplitudes, 'col', axis=1, tiled=True)]
    all_to_all x0 -> x1, starting transfers between devices: none -> 7.72 us  [on_device(): lax.all_to_all(jnp.stack([amplitudes] * lax.axis_size('col')), 'col', 0, 0)]
  transfers between devices with their start and end apart: 4 -> 4, of which waited for: 3 -> 4; matrix products, arithmetic and copies ran while one was open for 9% -> 4% of each run, Pallas kernels for 0% -> 0%
where the time goes in v1:
time: 616 us; the launch traced here: 613 us
  waiting for transfers between devices  419 us (68%)
  local copies, waits for them, and re-layouts  121 us (20%)
  other arithmetic  24.2 us (4%)
  matrix products  20.1 us (3%)
  starting transfers between devices  15.1 us (2%)
  between operations  13.6 us (2%)
    psum x1, waiting for transfers between devices, spread(): return lax.psum(block, axis)  143 us
    all_to_all x1, waiting for transfers between devices, on_device(): lax.all_to_all(jnp.stack([amplitudes] * lax.axis_size('col')), 'col', 0, 0)  119 us
    all_gather x1, waiting for transfers between devices, on_device(): residual_strip = lax.all_gather(cycle, 'col', axis=1, tiled=True)  87.4 us
    all_to_all x1, waiting for transfers between devices, on_device(): lax.all_to_all(packed, 'row', split_axis=2, concat_axis=0, tiled=True)  70.4 us
    another operation x1, local copies, waits for them, and re-layouts, on_device(): piece.reshape(occ_row, piece_count, slot_count, tile_width, tile_width)  40.1 us
    another operation x1, local copies, waits for them, and re-layouts, on_device(): received.reshape(piece_count, occ_col, slot_count, tile_width, tile_width)  20.6 us
    dot_general x1, matrix products, on_device(): jnp.einsum('iksac,kjscb->ijsab', left_tiles, right_tiles, preferred_eleme...  19 us
    gather x1, local copies, waits for them, and re-layouts, on_device(): packed = jnp.take(integrals, tile_second.reshape(-1), axis=2)  15.2 us
  transfers between devices with their start and end apart: 4, of which 4 were waited for; matrix products, arithmetic and copies ran while one was open for 4% of the time, Pallas kernels for 0%

profile of v1, /device:TPU:1, one launch (start us, length us, event | category | flops | bytes accessed | tf_op | source)
XLA Modules:
  0.0 613.4 jit_solution(7406031054567403025)
XLA Ops:
  6.5 0.9 fusion.29
  7.4 0.1 reshape_squeeze.6
  7.5 0.9 copy-done
  8.4 15.2 %gather_fusion = bf16[96,4,2,4096]{3,2,1,0:T(2,128)(2,1)} fusion(bf16[4,2,47,4096]{3,1,2,0:T(2,128)(2,1)S(1)} %copy-done, s32[1024]{0:T(1024)S(1)} %pad_clamp_fusion), kind=kCustom, calls=%fused_computation | custom fusion | bytes 12583296 | tf_op jit(solution)/shard_map/jit(_take)/gather | solution.py:25
  23.7 8.5 %broadcast_select_fusion.1 = bf16[4,2,8,12,4096]{4,1,3,0,2:T(2,128)(2,1)} fusion(pred[8,12]{1,0:T(8,128)(4,1)S(1)} %compare_and_fusion, bf16[4,2,8,12,4096]{4,1,0,3,2:T(2,128)(2,1)} %bitcast.66), kind=kLoop, calls=%fused_computation.5 | loop fusion | flops 3145728 | bytes 12583008 | tf_op jit(solution)/shard_map/jit(_take)/select_n | solution.py:25
  32.2 6.9 %all-to-all-start = ((bf16[4,2,8,12,4096]{4,1,3,0,2:T(2,128)(2,1)}), bf16[4,2,8,12,4096]{4,1,3,0,2:T(2,128)(2,1)}, u32[]{:S(2)}, u32[]{:S(2)}) async-start(bf16[4,2,8,12,4096]{4,1,3,0,2:T(2,128)(2,1)} %broadcast_select_fusion.1), calls=%async_computation | async-start | bytes 12582912 | tf_op jit(solution)/shard_map/all_to_all | solution.py:27
  39.1 0.8 copy.18
  39.9 70.4 %all-to-all-done = bf16[4,2,8,12,4096]{4,1,3,0,2:T(2,128)(2,1)} async-done(((bf16[4,2,8,12,4096]{4,1,3,0,2:T(2,128)(2,1)}), bf16[4,2,8,12,4096]{4,1,3,0,2:T(2,128)(2,1)}, u32[]{:S(2)}, u32[]{:S(2)}) %all-to-all-start) | async-done | bytes 6291488 | tf_op jit(solution)/shard_map/all_to_all | solution.py:27
  110.3 12.5 %stack.2 = bf16[16,4,2,12,4096]{4,2,1,3,0:T(2,128)(2,1)} broadcast(bf16[4,2,12,4096]{3,1,0,2:T(2,128)(2,1)S(1)} %copy.18), dimensions={1,2,3,4} | broadcast | bytes 13369344 | tf_op jit(solution)/shard_map/stack | solution.py:30
  122.7 7.7 %all-to-all-start.1 = ((bf16[16,4,2,12,4096]{4,2,1,3,0:T(2,128)(2,1)}), bf16[16,4,2,12,4096]{4,2,1,3,0:T(2,128)(2,1)}, u32[]{:S(2)}, u32[]{:S(2)}) async-start(bf16[16,4,2,12,4096]{4,2,1,3,0:T(2,128)(2,1)} %stack.2), calls=%async_computation.1 | async-start | bytes 25165824 | tf_op jit(solution)/shard_map/all_to_all | solution.py:30
  130.5 0.2 all-gather.2.cloned.1.call-start
  130.7 0.6 dynamic_slice.23
  131.3 0.6 compare_convert_fusion
  131.9 20.6 %reshape_reshape.6 = bf16[32,2,12,64,64]{4,3,1,2,0:T(8,128)(2,1)} reshape(bf16[8,4,2,1,12,4096]{5,2,4,1,0,3:T(2,128)(2,1)} %bitcast.5) | data formatting | bytes 12582912 | tf_op jit(solution)/shard_map/reshape;reshape | solution.py:34
  152.6 118.9 %all-to-all-done.1 = bf16[16,4,2,12,4096]{4,2,1,3,0:T(2,128)(2,1)} async-done(((bf16[16,4,2,12,4096]{4,2,1,3,0:T(2,128)(2,1)}), bf16[16,4,2,12,4096]{4,2,1,3,0:T(2,128)(2,1)}, u32[]{:S(2)}, u32[]{:S(2)}) %all-to-all-start.1) | async-done | bytes 12582944 | tf_op jit(solution)/shard_map/all_to_all | solution.py:30
  271.4 13.2 %copy.19 = bf16[4,16,2,12,4096]{4,2,1,0,3:T(2,128)(2,1)} copy(bf16[4,16,2,12,4096]{4,2,0,3,1:T(2,128)(2,1)} %bitcast.7) | data formatting | bytes 25165824 | tf_op jit(solution)/shard_map/reshape | solution.py:29
  284.7 40.1 %reshape.83 = bf16[4,32,12,64,64,1]{4,3,1,0,2,5:T(8,128)(2,1)} reshape(bf16[4,16,2,12,4096]{4,2,1,0,3:T(2,128)(2,1)} %copy.19) | data formatting | bytes 25165824 | tf_op jit(solution)/shard_map/reshape;reshape | solution.py:33
  324.8 19.0 %fusion.11 = bf16[4,2,12,64,64]{3,4,0,1,2:T(8,128)(2,1)S(1)} fusion(f32[12]{0:T(128)S(1)} %compare_convert_fusion, bf16[4,32,12,64,64,1]{4,3,1,0,2,5:T(8,128)(2,1)} %reshape.83, bf16[32,2,12,64,64]{4,3,1,2,0:T(8,128)(2,1)} %reshape_reshape.6), kind=kOutput, calls=%fused_computation.12 | convolution fusion | flops 1611399168 | bytes 19660848 | tf_op jit(solution)/shard_map/iksac,kjscb->ijsab/dot_general | solution.py:35
  343.8 1.8 copy.33
  345.6 3.7 reshape.87
  349.2 0.0 all-gather.2.cloned.1.call-update
  349.3 0.3 all-reduce.2.cloned.1.call-start
  349.6 87.4 %all-gather.2.cloned.1.call-done = bf16[4,32,12,4096]{3,0,2,1:T(4,128)(2,1)} async-done(((bf16[4,2,12,4096]{3,0,2,1:T(4,128)(2,1)}), bf16[4,32,12,4096]{3,0,2,1:T(4,128)(2,1)}) %all-gather.2.cloned.1.call-update) | async-done | bytes 12582928 | tf_op jit(solution)/shard_map/all_gather | solution.py:42
  437.0 10.8 %broadcast_select_fusion = bf16[2,32,12,4096]{3,0,2,1:T(2,128)(2,1)} fusion(pred[]{:T(512)S(6)} %eq.39, bf16[4,32,12,4096]{3,0,2,1:T(4,128)(2,1)} %all-gather.2.cloned.1.call-done, s32[]{:T(128)S(6)} %select_n.65), kind=kLoop, calls=%fused_computation.4 | loop fusion | flops 3145728 | bytes 12582917 | tf_op jit(solution)/shard_map/jit(_where)/select_n | solution.py:10
  447.7 0.0 all-reduce.2.cloned.1.call-update
  447.8 142.5 %all-reduce.2.cloned.1.call-done = bf16[2,32,12,4096]{3,0,2,1:T(2,128)(2,1)} async-done(((bf16[2,32,12,4096]{3,0,2,1:T(2,128)(2,1)}), bf16[2,32,12,4096]{3,0,2,1:T(2,128)(2,1)}) %all-reduce.2.cloned.1.call-update) | async-done | bytes 6291472 | tf_op jit(solution)/shard_map/psum | solution.py:11
  590.4 2.0 constant_dynamic-slice_fusion.4
  592.4 1.0 reshape.88
  593.4 1.1 fusion.5
  594.5 4.3 fusion.3
  598.8 3.6 copy.26
  602.4 4.2 reshape.73
  (14 shorter events, 0.1 us)
Async XLA Ops:
  6.5 1.9 copy-start
  32.2 6.9 %copy-start.3 = (bf16[4,2,12,4096]{3,1,2,0:T(2,128)(2,1)S(1)}, bf16[4,2,12,4096]{3,1,2,0:T(2,128)(2,1)}, u32[]{:S(2)}) copy-start(bf16[4,2,12,4096]{3,1,2,0:T(2,128)(2,1)} %param.4) | copy-start | bytes 2359300
  32.2 78.1 %all-to-all-start = ((bf16[4,2,8,12,4096]{4,1,3,0,2:T(2,128)(2,1)}), bf16[4,2,8,12,4096]{4,1,3,0,2:T(2,128)(2,1)}, u32[]{:S(2)}, u32[]{:S(2)}) async-start(bf16[4,2,8,12,4096]{4,1,3,0,2:T(2,128)(2,1)} %broadcast_select_fusion.1), calls=%async_computation | async-start | bytes 12582912 | tf_op jit(solution)/shard_map/all_to_all | solution.py:27
  122.7 8.0 %copy-start.4 = (s32[8]{0:T(128)S(1)}, s32[8]{0:T(128)}, u32[]{:S(2)}) copy-start(s32[8]{0:T(128)} %param.7) | copy-start | bytes 100
  122.7 148.7 %all-to-all-start.1 = ((bf16[16,4,2,12,4096]{4,2,1,3,0:T(2,128)(2,1)}), bf16[16,4,2,12,4096]{4,2,1,3,0:T(2,128)(2,1)}, u32[]{:S(2)}, u32[]{:S(2)}) async-start(bf16[16,4,2,12,4096]{4,2,1,3,0:T(2,128)(2,1)} %stack.2), calls=%async_computation.1 | async-start | bytes 25165824 | tf_op jit(solution)/shard_map/all_to_all | solution.py:30
  130.5 306.5 %all-gather.2.cloned.1.call-start = ((), (), s32[]{:S(2)}) async-start(), calls=%async_computation.2 | async-start | bytes 13369344 | tf_op jit(solution)/shard_map/all_gather | solution.py:42
  343.8 104.0 %copy-start.2 = (bf16[4,2,12,64,64]{3,4,0,1,2:T(8,128)(2,1)}, bf16[4,2,12,64,64]{3,4,0,1,2:T(8,128)(2,1)S(1)}, u32[]{:S(2)}) copy-start(bf16[4,2,12,64,64]{3,4,0,1,2:T(8,128)(2,1)S(1)} %fusion.11) | copy-start | bytes 2359300
  349.3 241.1 %all-reduce.2.cloned.1.call-start = ((), (), s32[]{:S(2)}) async-start(), calls=%async_computation.3 | async-start | bytes 12582912 | tf_op jit(solution)/shard_map/psum | solution.py:11
  594.5 12.0 %copy-start.1 = (bf16[4,2,47,4096]{3,1,2,0:T(2,128)(2,1)S(1)}, bf16[4,2,47,4096]{3,1,2,0:T(2,128)(2,1)}, u32[]{:S(2)}) copy-start(bf16[4,2,47,4096]{3,1,2,0:T(2,128)(2,1)} %param.5) | copy-start | bytes 9240580
Sparse Core Ops, SparseCore 0:
  349.4 87.5 all-gather.1
  447.9 142.4 all-reduce.1
